TPU v7x, 256 devices: a whole 4x4x8 slice. The times are simulated.
256 devices in a mesh: grp: 8 (over x, z_lo), dev: 32 (over y, z_hi, core).
Axes of the slice: x: 4, y: 4, z: 8 (z_hi: 4, z_lo: 2; z = z_hi * 2 + z_lo), core: 2. Of those that a mesh axis runs over, the one named last changes fastest.
Arguments:
- query: bfloat16 [512, 128, 4096], P(('grp', 'dev')), may hold values from -100 to 100
- grad_out: bfloat16 [512, 128, 4096], P(('grp', 'dev')), may hold values from -6 to 6
- branch_kv: bfloat16 [512, 128, 1024], P(('grp', 'dev')), may hold values from -6 to 6
- root_kv: bfloat16 [1024, 1024], P('dev'), may hold values from -24 to 24
- lengths: int32 [512], P(('grp', 'dev')), may hold values from 0 to 128, as said below
- segments: int32 [512], P(('grp', 'dev')), may hold values from 0 to 3
Outputs:
- query_grad: bfloat16 [512, 128, 4096], P(('grp', 'dev'))
- branch_grad: bfloat16 [512, 128, 1024], P(('grp', 'dev'))
- root_grad: float32 [1024, 1024], P('dev')
Inputs may be any that keep to these rules, and one draw needn't show every extreme that they name: `lengths`: A slot with length 0 holds no branch. A device's slots with live positions come before its empty slots. Within a group, device d and device d + 32/2 (d < 16) hold exactly 2 slots with live positions together; a quarter of a group's devices hold 2 such slots and a quarter hold none.
All inputs are finite; a program needn't handle non-finite values.
Results may differ from a plain program's by a relative error of at most 0.0069.
Values may be sent and summed in bfloat16 or wider, within the bound.
A program may use at most 128 MiB of HBM per device.

v0:
```python
import jax
import jax.numpy as jnp
from jax import lax
from jax.sharding import PartitionSpec as P

H = 32
KVH = 4
DH = 128
SEGS = 4


def passed_along(block, axis, distance):
    devices = range(lax.axis_size(axis))
    route = [((i - distance) % len(devices), i) for i in devices]
    return lax.ppermute(block, axis, route)


def cut_along(x, dim, peers):
    dims = x.shape
    blocks = x.reshape(*dims[:dim], peers, dims[dim] // peers, *dims[dim + 1 :])
    return jnp.moveaxis(blocks, dim, 0)


def summed_on_arrival(x, axis, dim):
    blocks = cut_along(x, dim, lax.axis_size(axis))
    arrived = lax.all_to_all(blocks, axis, split_axis=0, concat_axis=0, tiled=True)
    return arrived.astype(jnp.float32).sum(axis=0)


def from_everyone(x, axis):
    copies = jnp.broadcast_to(x, (lax.axis_size(axis), *x.shape))
    return lax.all_to_all(copies, axis, split_axis=0, concat_axis=0, tiled=True)


def over_copies(x, axis):
    return from_everyone(x, axis).sum(axis=0)


def tile_grads(query, grad, branch, length, segment, root_keys):
    rows = query.shape[0]
    width = KVH * DH
    groups = H // KVH
    roots = root_keys.shape[0]
    everything = jnp.concatenate([root_keys, branch], axis=0)
    span = roots + rows
    scale = DH ** (-0.5)
    row_pos = lax.broadcasted_iota(jnp.int32, (rows, span), 0)
    col_pos = lax.broadcasted_iota(jnp.int32, (rows, span), 1)
    visible = jnp.where(
        col_pos < roots, col_pos < (segment + 1) * (roots // SEGS), col_pos - roots <= row_pos
    )
    live = lax.broadcasted_iota(jnp.int32, (rows, 1), 0) < length
    grad = jnp.where(live, grad, jnp.zeros_like(grad))
    dq_parts = []
    dk_parts = []
    dv_parts = []
    for head in range(KVH):
        q_head = query[:, head * groups * DH : (head + 1) * groups * DH].reshape(rows, groups, DH)
        g_head = grad[:, head * groups * DH : (head + 1) * groups * DH].reshape(rows, groups, DH)
        k_head = everything[:, head * DH : (head + 1) * DH]
        v_head = everything[:, width + head * DH : width + (head + 1) * DH]
        scores = (
            jnp.einsum("tgd,ld->gtl", q_head, k_head, preferred_element_type=jnp.float32) * scale
        )
        scores = jnp.where(visible[None], scores, jnp.float32(-1e30))
        peak = jnp.max(scores, axis=-1, keepdims=True)
        weights = jnp.exp(scores - peak)
        weights = weights / jnp.sum(weights, axis=-1, keepdims=True)
        probs = weights.astype(jnp.bfloat16)
        output = jnp.einsum("gtl,ld->tgd", probs, v_head, preferred_element_type=jnp.float32)
        delta = jnp.sum(g_head.astype(jnp.float32) * output, axis=-1)
        dv_parts.append(
            jnp.einsum("gtl,tgd->ld", probs, g_head, preferred_element_type=jnp.float32)
        )
        prob_grad = jnp.einsum("tgd,ld->gtl", g_head, v_head, preferred_element_type=jnp.float32)
        score_grad = (weights * (prob_grad - delta.T[:, :, None]) * scale).astype(jnp.bfloat16)
        dq_parts.append(
            jnp.einsum(
                "gtl,ld->tgd", score_grad, k_head, preferred_element_type=jnp.float32
            ).reshape(rows, groups * DH)
        )
        dk_parts.append(
            jnp.einsum("gtl,tgd->ld", score_grad, q_head, preferred_element_type=jnp.float32)
        )
    dq = jnp.concatenate(dq_parts, axis=1).astype(jnp.bfloat16)
    dkv = jnp.concatenate(dk_parts + dv_parts, axis=1)
    return (dq, dkv[roots:].astype(jnp.bfloat16), dkv[:roots])


def local(query, grad_out, branch_kv, root_kv, lengths, segments):
    root_keys = lax.all_gather(root_kv, "dev", axis=0, tiled=True)
    half = lax.axis_size("dev") // 2
    live_count = jnp.sum((lengths > 0).astype(jnp.int32))
    arrived = passed_along(
        (query[1], grad_out[1], branch_kv[1], lengths[1:], segments[1:]), "dev", half
    )
    resident = live_count > 0
    q_tile = jnp.where(resident, query[0], arrived[0])
    g_tile = jnp.where(resident, grad_out[0], arrived[1])
    b_tile = jnp.where(resident, branch_kv[0], arrived[2])
    length = jnp.where(resident, lengths[0], arrived[3][0])
    segment = jnp.where(resident, segments[0], arrived[4][0])
    dq, dbranch, total = tile_grads(q_tile, g_tile, b_tile, length, segment, root_keys)
    returned = passed_along((dq, dbranch), "dev", half)
    second = live_count > 1
    query_grad = jnp.stack(
        [
            jnp.where(resident, dq, jnp.zeros_like(dq)),
            jnp.where(second, returned[0], jnp.zeros_like(dq)),
        ]
    )
    branch_grad = jnp.stack(
        [
            jnp.where(resident, dbranch, jnp.zeros_like(dbranch)),
            jnp.where(second, returned[1], jnp.zeros_like(dbranch)),
        ]
    )
    within = summed_on_arrival(total.astype(jnp.bfloat16), "dev", 0)
    root_grad = over_copies(within, "grp")
    return (query_grad, branch_grad, root_grad)


def solution(mesh):
    placed = (
        P(("grp", "dev"), None, None),
        P(("grp", "dev"), None, None),
        P(("grp", "dev"), None, None),
        P("dev", None),
        P(("grp", "dev")),
        P(("grp", "dev")),
    )
    return jax.shard_map(
        local,
        mesh=mesh,
        in_specs=placed,
        out_specs=(P(("grp", "dev"), None, None), P(("grp", "dev"), None, None), P("dev", None)),
        check_vma=False,
    )
```

profile of v0, /device:TPU:8, one launch (start us, length us, event | category | flops | bytes accessed | tf_op | source)
XLA Modules:
  0.0 251.1 jit_solution(15265945719861936562)
XLA Ops:
  7.2 1.0 slice_bitcast_fusion
  8.2 2.4 collective-permute-start
  10.6 1.3 fusion.109
  11.9 1.2 collective-permute-start.1
  13.1 1.7 fusion.105
  14.8 1.3 copy.208
  16.2 2.3 collective-permute-start.2
  19.0 1.2 collective-permute-start.3
  20.3 1.7 fusion.106
  22.0 1.3 copy.210
  23.3 2.3 collective-permute-start.4
  29.4 1.2 fusion.45
  30.7 14.4 %collective-permute-done.3 = s32[1]{0:T(128)} collective-permute-done((s32[1]{0:T(128)}, s32[1]{0:T(128)}, u32[]{:S(2)}, u32[]{:S(2)}) %collective-permute-start.3) | collective-permute-done | bytes 36 | tf_op jit(solution)/shard_map/ppermute | solution.py:15
  46.4 1.0 bitcast_select_fusion.10
  47.6 0.9 fusion.107
  48.5 17.4 %collective-permute-done.4 = bf16[128,4096]{0,1:T(8,128)(2,1)} collective-permute-done((bf16[128,4096]{0,1:T(8,128)(2,1)}, bf16[128,4096]{0,1:T(8,128)(2,1)}, u32[]{:S(2)}, u32[]{:S(2)}) %collective-permute-start.4) | collective-permute-done | bytes 1048608 | tf_op jit(solution)/shard_map/ppermute | solution.py:15
  66.0 1.0 copy-done.15
  66.9 0.8 fusion.108
  67.7 29.8 %all-gather.2.cloned.1.call-done = bf16[1024,1024]{1,0:T(8,128)(2,1)} async-done(((bf16[32,1024]{1,0:T(8,128)(2,1)}), bf16[1024,1024]{1,0:T(8,128)(2,1)}) %all-gather.2.cloned.1.call-update) | async-done | bytes 2097168 | tf_op jit(solution)/shard_map/all_gather | solution.py:91
  97.5 2.3 fusion.47
  99.8 4.4 %exponential_reduce_fusion.3 = (f32[8,128]{1,0:T(8,128)}, f32[8,128,1152]{1,2,0:T(8,128)}) fusion(pred[128,1152]{0,1:T(8,128)(4,1)S(1)} %fusion.45, bf16[128,8,128]{0,2,1:T(8,128)(2,1)S(1)} %bitcast.302, bf16[1152,128]{1,0:T(8,128)(2,1)S(1)} %get-tuple-element.11), kind=kOutput, calls=%fused_computation.50 | convolution fusion | flops 306709632 | bytes 5427200 | tf_op jit(solution)/shard_map/sub | solution.py:67
  104.2 3.1 %fusion.40 = bf16[8,128,1152]{1,2,0:T(8,128)(2,1)S(1)} fusion(f32[8,128]{1,0:T(8,128)} %get-tuple-element.38, f32[8,128,1152]{1,2,0:T(8,128)} %get-tuple-element.39), kind=kLoop, calls=%fused_computation.77 | loop fusion | flops 2359296 | bytes 7081984 | tf_op jit(solution)/shard_map/convert_element_type | solution.py:69
  107.9 1.8 copy-done.20
  109.7 1.3 fusion.19
  111.0 1.6 fusion.31
  112.6 5.4 %exponential_reduce_fusion.2 = (f32[8,128]{1,0:T(8,128)}, f32[8,128,1152]{1,2,0:T(8,128)}) fusion(pred[128,1152]{0,1:T(8,128)(4,1)S(1)} %fusion.45, bf16[128,8,128]{0,2,1:T(8,128)(2,1)} %bitcast.300, bf16[1152,128]{1,0:T(8,128)(2,1)} %get-tuple-element.12), kind=kOutput, calls=%fused_computation.48 | convolution fusion | flops 306709632 | bytes 5427200 | tf_op jit(solution)/shard_map/sub | solution.py:67
  118.0 3.1 %fusion.41 = bf16[8,128,1152]{1,2,0:T(8,128)(2,1)S(1)} fusion(f32[8,128]{1,0:T(8,128)} %get-tuple-element.36, f32[8,128,1152]{1,2,0:T(8,128)} %get-tuple-element.37), kind=kLoop, calls=%fused_computation.78 | loop fusion | flops 2359296 | bytes 7081984 | tf_op jit(solution)/shard_map/convert_element_type | solution.py:69
  121.7 0.9 copy-done
  122.6 1.7 copy-done.21
  124.4 1.3 fusion.16
  125.7 1.5 fusion.30
  127.3 5.4 %exponential_reduce_fusion.1 = (f32[8,128]{1,0:T(8,128)}, f32[8,128,1152]{1,2,0:T(8,128)}) fusion(pred[128,1152]{0,1:T(8,128)(4,1)S(1)} %fusion.45, bf16[128,8,128]{0,2,1:T(8,128)(2,1)} %bitcast.298, bf16[1152,128]{1,0:T(8,128)(2,1)} %get-tuple-element.13), kind=kOutput, calls=%fused_computation.46 | convolution fusion | flops 306709632 | bytes 5427200 | tf_op jit(solution)/shard_map/sub | solution.py:67
  132.7 3.3 %fusion.42 = bf16[8,128,1152]{1,2,0:T(8,128)(2,1)S(1)} fusion(f32[8,128]{1,0:T(8,128)} %get-tuple-element.34, f32[8,128,1152]{1,2,0:T(8,128)} %get-tuple-element.35), kind=kLoop, calls=%fused_computation.79 | loop fusion | flops 2359296 | bytes 7081984 | tf_op jit(solution)/shard_map/convert_element_type | solution.py:69
  136.6 0.8 copy-done.2
  137.4 1.8 copy-done.19
  139.2 1.3 fusion.13
  140.6 1.6 fusion.29
  142.2 5.3 %exponential_reduce_fusion = (f32[8,128]{1,0:T(8,128)}, f32[8,128,1152]{1,2,0:T(8,128)}) fusion(pred[128,1152]{0,1:T(8,128)(4,1)S(1)} %fusion.45, bf16[128,8,128]{0,2,1:T(8,128)(2,1)S(1)} %bitcast.296, bf16[1152,128]{1,0:T(8,128)(2,1)} %get-tuple-element.15), kind=kOutput, calls=%fused_computation.44 | convolution fusion | flops 306709632 | bytes 5427200 | tf_op jit(solution)/shard_map/sub | solution.py:67
  147.5 3.1 %fusion.43 = bf16[8,128,1152]{1,2,0:T(8,128)(2,1)S(1)} fusion(f32[8,128]{1,0:T(8,128)} %get-tuple-element.32, f32[8,128,1152]{1,2,0:T(8,128)} %get-tuple-element.33), kind=kLoop, calls=%fused_computation.80 | loop fusion | flops 2359296 | bytes 7081984 | tf_op jit(solution)/shard_map/convert_element_type | solution.py:69
  150.7 1.5 multiply_reduce_fusion
  152.3 1.3 fusion.10
  153.9 0.9 fusion.28
  155.4 0.9 fusion.27
  156.3 0.8 copy-done.1
  157.0 0.9 fusion.26
  157.9 0.8 copy-done.3
  158.7 0.9 fusion.25
  159.6 0.9 fusion.24
  160.5 1.6 slice.137
  162.6 7.3 %all-to-all-start = ((bf16[32,32,1024]{2,1,0:T(8,128)(2,1)}), bf16[32,32,1024]{2,1,0:T(8,128)(2,1)}, u32[]{:S(2)}, u32[]{:S(2)}) async-start(bf16[32,32,1024]{2,1,0:T(8,128)(2,1)} %bitcast.275), calls=%async_computation | async-start | bytes 4194304 | tf_op jit(solution)/shard_map/all_to_all | solution.py:26
  170.6 1.9 select_bitcast_fusion.2
  172.5 2.1 collective-permute-start.6
  174.6 1.5 convolution_convert_fusion.3
  178.4 1.1 pad_maximum_fusion.1
  179.5 1.4 collective-permute-start.5
  180.9 38.8 %all-to-all-done = bf16[32,32,1024]{2,1,0:T(8,128)(2,1)} async-done(((bf16[32,32,1024]{2,1,0:T(8,128)(2,1)}), bf16[32,32,1024]{2,1,0:T(8,128)(2,1)}, u32[]{:S(2)}, u32[]{:S(2)}) %all-to-all-start) | async-done | bytes 2097184 | tf_op jit(solution)/shard_map/all_to_all | solution.py:26
  219.7 2.0 convert_reduce_fusion
  221.6 1.1 broadcast_in_dim.54
  222.7 4.3 %all-to-all-start.1 = ((f32[8,32,1024]{2,1,0:T(8,128)}), f32[8,32,1024]{2,1,0:T(8,128)S(1)}, u32[]{:S(2)}, u32[]{:S(2)}) async-start(f32[8,32,1024]{2,1,0:T(8,128)} %broadcast_in_dim.54), calls=%async_computation.1 | async-start | bytes 2097152 | tf_op jit(solution)/shard_map/all_to_all | solution.py:32
  227.2 0.7 copy-done.27
  227.9 0.8 pad_maximum_fusion.2
  229.0 2.7 %copy.150 = bf16[2,128,4096]{2,1,0:T(8,128)(2,1)} copy(bf16[2,128,4096]{1,2,0:T(8,128)(2,1)S(1)} %pad_maximum_fusion) | data formatting | bytes 4194304
  231.8 11.7 %all-to-all-done.1 = f32[8,32,1024]{2,1,0:T(8,128)S(1)} async-done(((f32[8,32,1024]{2,1,0:T(8,128)}), f32[8,32,1024]{2,1,0:T(8,128)S(1)}, u32[]{:S(2)}, u32[]{:S(2)}) %all-to-all-start.1) | async-done | bytes 1048608 | tf_op jit(solution)/shard_map/all_to_all | solution.py:32
  243.5 0.7 reduce_sum.109
  (97 shorter events, 8.6 us)
Async XLA Ops:
  7.2 90.3 %all-gather.2.cloned.1.call-start = ((), (), s32[]{:S(2)}) async-start(), calls=%async_computation.2 | async-start | bytes 2162688 | tf_op jit(solution)/shard_map/all_gather | solution.py:91
  8.2 38.2 %collective-permute-start = (bf16[128,1024]{1,0:T(8,128)(2,1)S(1)}, bf16[128,1024]{1,0:T(8,128)(2,1)}, u32[]{:S(2)}, u32[]{:S(2)}) collective-permute-start(bf16[128,1024]{1,0:T(8,128)(2,1)S(1)} %slice_bitcast_fusion), channel_id=1, source_target_pairs={{16,0},{17,1},{18,2},{19,3},{20,4},{21,5},{22,6},{23,7},{24,8},{25... | collective-permute-start | bytes 786440 | tf_op jit(solution)/shard_map/ppermute | solution.py:15
  11.9 6.5 %copy-start.39 = (s32[2]{0:T(128)S(1)}, s32[2]{0:T(128)}, u32[]{:S(2)}) copy-start(s32[2]{0:T(128)} %param.10) | copy-start | bytes 28
  11.9 16.3 %collective-permute-start.1 = (s32[1]{0:T(128)}, s32[1]{0:T(128)}, u32[]{:S(2)}, u32[]{:S(2)}) collective-permute-start(s32[1]{0:T(128)} %get-tuple-element.28), channel_id=1, source_target_pairs={{16,0},{17,1},{18,2},{19,3},{20,4},{21,5},{22,6},{23,7},{24,8},{25... | collective-permute-start | bytes 20 | tf_op jit(solution)/shard_map/ppermute | solution.py:15
  16.2 31.3 %collective-permute-start.2 = (bf16[128,4096]{0,1:T(8,128)(2,1)}, bf16[128,4096]{0,1:T(8,128)(2,1)}, u32[]{:S(2)}, u32[]{:S(2)}) collective-permute-start(bf16[128,4096]{0,1:T(8,128)(2,1)} %bitcast.7), channel_id=1, source_target_pairs={{16,0},{17,1},{18,2},{19,3},{20,4},{21,5},{22,6},{23,7},{24,8},{25... | collective-permute-start | bytes 3145736 | tf_op jit(solution)/shard_map/ppermute | solution.py:15
  19.0 26.0 %collective-permute-start.3 = (s32[1]{0:T(128)}, s32[1]{0:T(128)}, u32[]{:S(2)}, u32[]{:S(2)}) collective-permute-start(s32[1]{0:T(128)} %get-tuple-element.30), channel_id=1, source_target_pairs={{16,0},{17,1},{18,2},{19,3},{20,4},{21,5},{22,6},{23,7},{24,8},{25... | collective-permute-start | bytes 20 | tf_op jit(solution)/shard_map/ppermute | solution.py:15
  23.3 42.6 %collective-permute-start.4 = (bf16[128,4096]{0,1:T(8,128)(2,1)}, bf16[128,4096]{0,1:T(8,128)(2,1)}, u32[]{:S(2)}, u32[]{:S(2)}) collective-permute-start(bf16[128,4096]{0,1:T(8,128)(2,1)} %bitcast.293), channel_id=1, source_target_pairs={{16,0},{17,1},{18,2},{19,3},{20,4},{21,5},{22,6},{23,7},{24,8},{25... | collective-permute-start | bytes 3145736 | tf_op jit(solution)/shard_map/ppermute | solution.py:15
  48.5 51.3 %copy-start.33 = (bf16[128,1024]{0,1:T(8,128)(2,1)}, bf16[128,1024]{0,1:T(8,128)(2,1)S(1)}, u32[]{:S(2)}) copy-start(bf16[128,1024]{0,1:T(8,128)(2,1)S(1)} %get-tuple-element.20) | copy-start | bytes 786436
  66.0 1.0 copy-start.15
  99.8 4.4 %copy-start.25 = (bf16[1152,128]{1,0:T(8,128)(2,1)}, bf16[1152,128]{1,0:T(8,128)(2,1)S(1)}, u32[]{:S(2)}) copy-start(bf16[1152,128]{1,0:T(8,128)(2,1)S(1)} %get-tuple-element.11) | copy-start | bytes 884740
  104.2 3.1 %copy-start.4 = (bf16[1024,1024]{1,0:T(8,128)(2,1)S(1)}, bf16[1024,1024]{1,0:T(8,128)(2,1)}, u32[]{:S(2)}) copy-start(bf16[1024,1024]{1,0:T(8,128)(2,1)} %all-gather.2.cloned.1.call-done) | copy-start | bytes 6291460
  107.3 2.3 copy-start.20
  107.4 2.3 copy-start.37
  109.7 1.3 copy-start.34
  111.0 1.6 copy-start.7
  118.0 3.1 %copy-start.5 = (bf16[1024,1024]{1,0:T(8,128)(2,1)S(1)}, bf16[1024,1024]{1,0:T(8,128)(2,1)}, u32[]{:S(2)}) copy-start(bf16[1024,1024]{1,0:T(8,128)(2,1)} %all-gather.2.cloned.1.call-done) | copy-start | bytes 6291460
  121.2 1.5 copy-start
  121.2 3.2 %copy-start.21 = (f32[8,128,1152]{1,2,0:T(8,128)S(1)}, f32[8,128,1152]{1,2,0:T(8,128)}, u32[]{:S(2)}) copy-start(f32[8,128,1152]{1,2,0:T(8,128)} %get-tuple-element.37) | copy-start | bytes 14155780
  121.2 3.2 %copy-start.38 = (f32[8,128]{1,0:T(8,128)S(1)}, f32[8,128]{1,0:T(8,128)}, u32[]{:S(2)}) copy-start(f32[8,128]{1,0:T(8,128)} %get-tuple-element.36) | copy-start | bytes 12292
  124.4 1.3 copy-start.32
  125.7 1.5 copy-start.9
  132.7 3.4 %copy-start.6 = (bf16[1024,1024]{1,0:T(8,128)(2,1)S(1)}, bf16[1024,1024]{1,0:T(8,128)(2,1)}, u32[]{:S(2)}) copy-start(bf16[1024,1024]{1,0:T(8,128)(2,1)} %all-gather.2.cloned.1.call-done) | copy-start | bytes 6291460
  136.0 1.4 copy-start.2
  136.0 3.2 %copy-start.19 = (f32[8,128,1152]{1,2,0:T(8,128)S(1)}, f32[8,128,1152]{1,2,0:T(8,128)}, u32[]{:S(2)}) copy-start(f32[8,128,1152]{1,2,0:T(8,128)} %get-tuple-element.35) | copy-start | bytes 14155780
  136.0 3.2 %copy-start.36 = (f32[8,128]{1,0:T(8,128)S(1)}, f32[8,128]{1,0:T(8,128)}, u32[]{:S(2)}) copy-start(f32[8,128]{1,0:T(8,128)} %get-tuple-element.34) | copy-start | bytes 12292
  139.2 1.3 copy-start.31
  140.6 1.6 copy-start.11
  140.6 1.6 copy-start.29
  147.5 3.2 %copy-start.26 = (bf16[1152,128,1]{1,0,2:T(8,128)(2,1)S(1)}, bf16[1152,128,1]{1,0,2:T(8,128)(2,1)}, u32[]{:S(2)}) copy-start(bf16[1152,128,1]{1,0,2:T(8,128)(2,1)} %get-tuple-element.14) | copy-start | bytes 884740
  147.5 4.7 %copy-start.18 = (f32[8,128,1152]{1,2,0:T(8,128)S(1)}, f32[8,128,1152]{1,2,0:T(8,128)}, u32[]{:S(2)}) copy-start(f32[8,128,1152]{1,2,0:T(8,128)} %get-tuple-element.33) | copy-start | bytes 14155780
  150.6 1.6 copy-start.28
  150.6 1.6 copy-start.35
  152.2 1.7 copy-start.16
  152.2 1.7 copy-start.30
  153.9 1.4 copy-start.13
  155.4 1.7 copy-start.1
  157.0 1.7 copy-start.3
  160.5 2.1 copy-start.17
  162.6 12.0 %copy-start.8 = (bf16[8,128,1152]{1,2,0:T(8,128)(2,1)S(1)}, bf16[8,128,1152]{1,2,0:T(8,128)(2,1)}, u32[]{:S(2)}) copy-start(bf16[8,128,1152]{1,2,0:T(8,128)(2,1)} %copy-done.7) | copy-start | bytes 7077892
  162.6 57.0 %all-to-all-start = ((bf16[32,32,1024]{2,1,0:T(8,128)(2,1)}), bf16[32,32,1024]{2,1,0:T(8,128)(2,1)}, u32[]{:S(2)}, u32[]{:S(2)}) async-start(bf16[32,32,1024]{2,1,0:T(8,128)(2,1)} %bitcast.275), calls=%async_computation | async-start | bytes 4194304 | tf_op jit(solution)/shard_map/all_to_all | solution.py:26
  169.9 6.2 %copy-start.24 = (bf16[1152,128]{1,0:T(8,128)(2,1)S(1)}, bf16[1152,128]{1,0:T(8,128)(2,1)}, u32[]{:S(2)}) copy-start(bf16[1152,128]{1,0:T(8,128)(2,1)} %get-tuple-element.12) | copy-start | bytes 884740
  170.6 5.6 %copy-start.10 = (bf16[8,128,1152]{1,2,0:T(8,128)(2,1)S(1)}, bf16[8,128,1152]{1,2,0:T(8,128)(2,1)}, u32[]{:S(2)}) copy-start(bf16[8,128,1152]{1,2,0:T(8,128)(2,1)} %copy-done.9) | copy-start | bytes 7077892
  172.5 4.2 %copy-start.12 = (bf16[8,128,1152]{1,2,0:T(8,128)(2,1)S(1)}, bf16[8,128,1152]{1,2,0:T(8,128)(2,1)}, u32[]{:S(2)}) copy-start(bf16[8,128,1152]{1,2,0:T(8,128)(2,1)} %copy-done.11) | copy-start | bytes 7077892
  172.5 4.2 %copy-start.23 = (bf16[1152,128]{1,0:T(8,128)(2,1)S(1)}, bf16[1152,128]{1,0:T(8,128)(2,1)}, u32[]{:S(2)}) copy-start(bf16[1152,128]{1,0:T(8,128)(2,1)} %get-tuple-element.13) | copy-start | bytes 884740
  172.5 54.7 %collective-permute-start.6 = (bf16[128,1024]{1,0:T(8,128)(2,1)}, bf16[128,1024]{1,0:T(8,128)(2,1)}, u32[]{:S(2)}, u32[]{:S(2)}) collective-permute-start(bf16[128,1024]{1,0:T(8,128)(2,1)} %get-tuple-element.10), channel_id=1, source_target_pairs={{16,0},{17,1},{18,2},{19,3},{20,4},{21,5},{22,6},{23,7},{24,8},{25... | collective-permute-start | bytes 786440 | tf_op jit(solution)/shard_map/ppermute | solution.py:15
  176.2 1.7 copy-start.14
  176.2 1.7 copy-start.22
  179.5 49.3 %collective-permute-start.5 = (bf16[128,4096]{0,1:T(8,128)(2,1)}, bf16[128,4096]{0,1:T(8,128)(2,1)S(1)}, u32[]{:S(2)}, u32[]{:S(2)}) collective-permute-start(bf16[128,4096]{0,1:T(8,128)(2,1)} %pad_maximum_fusion.1), channel_id=1, source_target_pairs={{16,0},{17,1},{18,2},{19,3},{20,4},{21,5},{22,6},{23,7},{24,8},{25... | collective-permute-start | bytes 3145736 | tf_op jit(solution)/shard_map/ppermute | solution.py:15
  222.7 20.8 %all-to-all-start.1 = ((f32[8,32,1024]{2,1,0:T(8,128)}), f32[8,32,1024]{2,1,0:T(8,128)S(1)}, u32[]{:S(2)}, u32[]{:S(2)}) async-start(f32[8,32,1024]{2,1,0:T(8,128)} %broadcast_in_dim.54), calls=%async_computation.1 | async-start | bytes 2097152 | tf_op jit(solution)/shard_map/all_to_all | solution.py:32
  227.0 0.9 copy-start.27
Sparse Core Ops, SparseCore 0:
  10.7 86.7 all-gather.1
where the time goes:
time: 252 us; the launch traced here: 251 us
  waiting for transfers between devices  112 us (44%)
  matrix products  41.3 us (16%)
  local copies, waits for them, and re-layouts  29.5 us (12%)
  other arithmetic  25.2 us (10%)
  starting transfers between devices  24.5 us (10%)
  between operations  18.5 us (7%)
    all_to_all x1, waiting for transfers between devices, summed_on_arrival(): lax.all_to_all(blocks, axis, split_axis=0, concat_axis=0, tiled=True)  38.8 us
    ppermute x7, waiting for transfers between devices, passed_along(): return lax.ppermute(block, axis, route)  31.7 us
    all_gather x1, waiting for transfers between devices, local(): root_keys = lax.all_gather(root_kv, 'dev', axis=0, tiled=True)  29.8 us
    sub x4, matrix products, tile_grads(): weights = jnp.exp(scores - peak)  20.5 us
    unnamed x85, local copies, waits for them, and re-layouts  18.8 us
    ppermute x7, starting transfers between devices, passed_along(): return lax.ppermute(block, axis, route)  13 us
    convert_element_type x4, other arithmetic, tile_grads(): probs = weights.astype(jnp.bfloat16)  12.7 us
    all_to_all x1, waiting for transfers between devices, from_everyone(): return lax.all_to_all(copies, axis, split_axis=0, concat_axis=0, tiled=True)  11.7 us
  transfers between devices with their start and end apart: 10, of which 5 were waited for; matrix products, arithmetic and copies ran while one was open for 11% of the time, Pallas kernels for 0%

commit v1 on v0

--- a/solution.py
+++ b/solution.py
@@ -88,7 +88,9 @@
 
 
 def local(query, grad_out, branch_kv, root_kv, lengths, segments):
-    root_keys = lax.all_gather(root_kv, "dev", axis=0, tiled=True)
+    root_keys = jnp.concatenate(
+        lax.all_to_all(jnp.stack([root_kv] * lax.axis_size("dev")), "dev", 0, 0), axis=0
+    )
     half = lax.axis_size("dev") // 2
     live_count = jnp.sum((lengths > 0).astype(jnp.int32))
     arrived = passed_along(

time: 252 us -> 256 us (1.016)
  starting transfers between devices: 24.5 us -> 39.4 us
  between operations: 18.5 us -> 4.9 us
  local copies, waits for them, and re-layouts: 29.5 us -> 42.6 us
  waiting for transfers between devices: 112 us -> 103 us
    all_gather x1 -> x0, waiting for transfers between devices: 29.8 us -> none  [local(): root_keys = lax.all_gather(root_kv, 'dev', axis=0, tiled=True)]
    ppermute x7, waiting for transfers between devices: 31.7 us -> 52.6 us  [passed_along(): return lax.ppermute(block, axis, route)]
    all_to_all x0 -> x1, starting transfers between devices: none -> 10.5 us  [local(): lax.all_to_all(jnp.stack([root_kv] * lax.axis_size('dev')), 'dev', 0, 0)]
    unnamed x85 -> x111, local copies, waits for them, and re-layouts: 18.8 us -> 26.9 us
    all_to_all x1, starting transfers between devices: 7.26 us -> 11.5 us  [summed_on_arrival(): lax.all_to_all(blocks, axis, split_axis=0, concat_axis=0, tiled=True)]
  transfers between devices with their start and end apart: 10 -> 10, of which waited for: 5 -> 3; matrix products, arithmetic and copies ran while one was open for 11% -> 15% of each run, Pallas kernels for 0% -> 0%
where the time goes in v1:
time: 256 us; the launch traced here: 255 us
  waiting for transfers between devices  103 us (40%)
  local copies, waits for them, and re-layouts  42.6 us (17%)
  matrix products  40 us (16%)
  starting transfers between devices  39.4 us (15%)
  other arithmetic  25.3 us (10%)
  between operations  4.9 us (2%)
    ppermute x7, waiting for transfers between devices, passed_along(): return lax.ppermute(block, axis, route)  52.6 us
    all_to_all x1, waiting for transfers between devices, summed_on_arrival(): lax.all_to_all(blocks, axis, split_axis=0, concat_axis=0, tiled=True)  38.9 us
    unnamed x111, local copies, waits for them, and re-layouts  26.9 us
    sub x4, matrix products, tile_grads(): weights = jnp.exp(scores - peak)  20 us
    ppermute x7, starting transfers between devices, passed_along(): return lax.ppermute(block, axis, route)  13 us
    convert_element_type x4, other arithmetic, tile_grads(): probs = weights.astype(jnp.bfloat16)  12.4 us
    all_to_all x1, starting transfers between devices, summed_on_arrival(): lax.all_to_all(blocks, axis, split_axis=0, concat_axis=0, tiled=True)  11.5 us
    all_to_all x1, waiting for transfers between devices, from_everyone(): return lax.all_to_all(copies, axis, split_axis=0, concat_axis=0, tiled=True)  11.2 us
  transfers between devices with their start and end apart: 10, of which 3 were waited for; matrix products, arithmetic and copies ran while one was open for 15% of the time, Pallas kernels for 0%

profile of v1, /device:TPU:8, one launch (start us, length us, event | category | flops | bytes accessed | tf_op | source)
XLA Modules:
  0.0 254.9 jit_solution(5021201688280797955)
XLA Ops:
  0.6 1.3 fusion.110
  1.9 2.3 collective-permute-start.3
  4.2 2.4 stack.12
  6.7 10.5 %all-to-all-start = ((bf16[32,32,1024]{2,1,0:T(8,128)(2,1)}), bf16[32,32,1024]{2,1,0:T(8,128)(2,1)S(1)}, u32[]{:S(2)}, u32[]{:S(2)}) async-start(bf16[32,32,1024]{2,1,0:T(8,128)(2,1)} %stack.12), calls=%async_computation | async-start | bytes 4194304 | tf_op jit(solution)/shard_map/all_to_all | solution.py:92
  17.1 2.7 %fusion.105 = (bf16[1,128,4096]{2,1,0:T(8,128)(2,1)S(1)}, bf16[1,128,4096]{2,1,0:T(8,128)(2,1)}) fusion(bf16[2,128,4096]{2,1,0:T(8,128)(2,1)} %param.6), kind=kLoop, calls=%fused_computation.154 | loop fusion | bytes 4194304 | tf_op jit(solution)/shard_map/slice | solution.py:100
  19.9 2.3 copy.208
  22.1 2.1 collective-permute-start.2
  24.2 3.1 %fusion.106 = (bf16[1,128,4096]{2,1,0:T(8,128)(2,1)}, bf16[1,128,4096]{2,1,0:T(8,128)(2,1)}) fusion(bf16[2,128,4096]{2,1,0:T(8,128)(2,1)} %param.7), kind=kLoop, calls=%fused_computation.155 | loop fusion | bytes 4194304 | tf_op jit(solution)/shard_map/slice | solution.py:101
  27.3 2.3 copy.210
  29.6 1.4 collective-permute-start.4
  31.0 1.0 slice_bitcast_fusion
  32.0 2.2 collective-permute-start
  34.7 1.4 collective-permute-start.1
  36.8 1.3 copy.207
  38.1 2.3 copy.209
  41.1 52.6 %collective-permute-done.1 = s32[1]{0:T(128)} collective-permute-done((s32[1]{0:T(128)}, s32[1]{0:T(128)}, u32[]{:S(2)}, u32[]{:S(2)}) %collective-permute-start.1) | collective-permute-done | bytes 36 | tf_op jit(solution)/shard_map/ppermute | solution.py:15
  94.8 1.2 fusion.45
  97.5 1.8 fusion.44
  99.2 1.0 fusion.107
  100.2 1.0 fusion.108
  101.2 1.2 fusion.47
  102.4 5.4 %exponential_reduce_fusion.3 = (f32[8,128]{1,0:T(8,128)}, f32[8,128,1152]{1,2,0:T(8,128)}) fusion(pred[128,1152]{0,1:T(8,128)(4,1)S(1)} %fusion.45, bf16[128,8,128]{0,2,1:T(8,128)(2,1)} %bitcast.311, bf16[1152,128]{1,0:T(8,128)(2,1)} %get-tuple-element.11), kind=kOutput, calls=%fused_computation.50 | convolution fusion | flops 306709632 | bytes 5427200 | tf_op jit(solution)/shard_map/sub | solution.py:67
  107.9 3.0 %fusion.40 = bf16[8,128,1152]{1,2,0:T(8,128)(2,1)S(1)} fusion(f32[8,128]{1,0:T(8,128)} %get-tuple-element.38, f32[8,128,1152]{1,2,0:T(8,128)} %get-tuple-element.39), kind=kLoop, calls=%fused_computation.77 | loop fusion | flops 2359296 | bytes 7081984 | tf_op jit(solution)/shard_map/convert_element_type | solution.py:69
  111.5 0.8 copy-done
  112.3 1.8 copy-done.20
  114.1 1.3 fusion.19
  115.4 1.5 fusion.31
  117.0 5.4 %exponential_reduce_fusion.2 = (f32[8,128]{1,0:T(8,128)}, f32[8,128,1152]{1,2,0:T(8,128)}) fusion(pred[128,1152]{0,1:T(8,128)(4,1)S(1)} %fusion.45, bf16[128,8,128]{0,2,1:T(8,128)(2,1)} %bitcast.309, bf16[1152,128]{1,0:T(8,128)(2,1)} %get-tuple-element.12), kind=kOutput, calls=%fused_computation.48 | convolution fusion | flops 306709632 | bytes 5427200 | tf_op jit(solution)/shard_map/sub | solution.py:67
  122.4 3.0 %fusion.41 = bf16[8,128,1152]{1,2,0:T(8,128)(2,1)S(1)} fusion(f32[8,128]{1,0:T(8,128)} %get-tuple-element.36, f32[8,128,1152]{1,2,0:T(8,128)} %get-tuple-element.37), kind=kLoop, calls=%fused_computation.78 | loop fusion | flops 2359296 | bytes 7081984 | tf_op jit(solution)/shard_map/convert_element_type | solution.py:69
  126.0 0.8 copy-done.2
  126.8 1.8 copy-done.21
  128.6 2.9 %fusion.16 = bf16[8,128,1152]{1,2,0:T(8,128)(2,1)} fusion(bf16[128,8,128]{0,2,1:T(8,128)(2,1)S(1)} %bitcast.296, f32[8,128]{1,0:T(8,128)S(1)} %bitcast.316, f32[8,128]{1,0:T(8,128)S(1)} %copy-done.50, f32[8,128,1152]{1,2,0:T(8,128)S(1)} %copy-done.21, bf16[1024,1024]{1,0:T(8,128)(2,1)S(1)} %bitcast.280, bf16[128,1024]{1,0:T(8,128)(2,1)S(1)} %bitcast_select_fusion.10), kind=kOutput, calls=%fused_computation.32 | convolution fusion | flops 308477952 | bytes 9707520 | tf_op jit(solution)/shard_map/tgd,ld->gtl/dot_general | solution.py:75
  131.5 5.4 %exponential_reduce_fusion.1 = (f32[8,128]{1,0:T(8,128)}, f32[8,128,1152]{1,2,0:T(8,128)}) fusion(pred[128,1152]{0,1:T(8,128)(4,1)S(1)} %fusion.45, bf16[128,8,128]{0,2,1:T(8,128)(2,1)} %bitcast.307, bf16[1152,128]{1,0:T(8,128)(2,1)} %get-tuple-element.13), kind=kOutput, calls=%fused_computation.46 | convolution fusion | flops 306709632 | bytes 5427200 | tf_op jit(solution)/shard_map/sub | solution.py:67
  136.9 3.2 %fusion.42 = bf16[8,128,1152]{1,2,0:T(8,128)(2,1)S(1)} fusion(f32[8,128]{1,0:T(8,128)} %get-tuple-element.34, f32[8,128,1152]{1,2,0:T(8,128)} %get-tuple-element.35), kind=kLoop, calls=%fused_computation.79 | loop fusion | flops 2359296 | bytes 7081984 | tf_op jit(solution)/shard_map/convert_element_type | solution.py:69
  140.7 0.8 copy-done.4
  141.6 1.8 copy-done.19
  143.4 1.3 fusion.13
  145.7 0.9 fusion.30
  147.1 0.9 fusion.29
  148.0 1.4 copy-done.15
  149.4 3.8 %exponential_reduce_fusion = (f32[8,128]{1,0:T(8,128)S(1)}, f32[8,128,1152]{1,2,0:T(8,128)}) fusion(pred[128,1152]{0,1:T(8,128)(4,1)S(1)} %fusion.45, bf16[128,8,128]{0,2,1:T(8,128)(2,1)S(1)} %bitcast.305, bf16[1152,128]{1,0:T(8,128)(2,1)S(1)} %copy-done.33), kind=kOutput, calls=%fused_computation.44 | convolution fusion | flops 306709632 | bytes 5427200 | tf_op jit(solution)/shard_map/sub | solution.py:67
  153.2 3.1 %fusion.43 = bf16[8,128,1152]{1,2,0:T(8,128)(2,1)S(1)} fusion(f32[8,128]{1,0:T(8,128)S(1)} %get-tuple-element.32, f32[8,128,1152]{1,2,0:T(8,128)} %get-tuple-element.33), kind=kLoop, calls=%fused_computation.80 | loop fusion | flops 2359296 | bytes 7081984 | tf_op jit(solution)/shard_map/convert_element_type | solution.py:69
  157.5 1.3 fusion.10
  159.2 0.9 fusion.28
  160.6 1.1 copy-done.1
  161.7 0.9 fusion.27
  163.3 0.9 fusion.26
  165.0 0.9 fusion.25
  165.9 0.9 fusion.24
  166.8 1.6 slice.137
  168.9 11.5 %all-to-all-start.1 = ((bf16[32,32,1024]{2,1,0:T(8,128)(2,1)}), bf16[32,32,1024]{2,1,0:T(8,128)(2,1)}, u32[]{:S(2)}, u32[]{:S(2)}) async-start(bf16[32,32,1024]{2,1,0:T(8,128)(2,1)} %bitcast.283), calls=%async_computation.1 | async-start | bytes 4194304 | tf_op jit(solution)/shard_map/all_to_all | solution.py:26
  181.1 1.9 select_bitcast_fusion.2
  183.1 2.1 collective-permute-start.6
  185.2 1.5 convolution_convert_fusion.3
  189.1 1.1 pad_maximum_fusion.1
  190.1 1.4 collective-permute-start.5
  191.5 38.9 %all-to-all-done.1 = bf16[32,32,1024]{2,1,0:T(8,128)(2,1)} async-done(((bf16[32,32,1024]{2,1,0:T(8,128)(2,1)}), bf16[32,32,1024]{2,1,0:T(8,128)(2,1)}, u32[]{:S(2)}, u32[]{:S(2)}) %all-to-all-start.1) | async-done | bytes 2097184 | tf_op jit(solution)/shard_map/all_to_all | solution.py:26
  230.4 2.0 convert_reduce_fusion
  232.4 1.1 broadcast_in_dim.54
  233.5 4.4 %all-to-all-start.2 = ((f32[8,32,1024]{2,1,0:T(8,128)}), f32[8,32,1024]{2,1,0:T(8,128)S(1)}, u32[]{:S(2)}, u32[]{:S(2)}) async-start(f32[8,32,1024]{2,1,0:T(8,128)} %broadcast_in_dim.54), calls=%async_computation.2 | async-start | bytes 2097152 | tf_op jit(solution)/shard_map/all_to_all | solution.py:32
  237.9 1.2 maximum_select_fusion
  239.1 0.8 pad_maximum_fusion.2
  240.3 2.7 %copy.150 = bf16[2,128,4096]{2,1,0:T(8,128)(2,1)} copy(bf16[2,128,4096]{1,2,0:T(8,128)(2,1)S(1)} %pad_maximum_fusion) | data formatting | bytes 4194304
  243.0 11.2 %all-to-all-done.2 = f32[8,32,1024]{2,1,0:T(8,128)S(1)} async-done(((f32[8,32,1024]{2,1,0:T(8,128)}), f32[8,32,1024]{2,1,0:T(8,128)S(1)}, u32[]{:S(2)}, u32[]{:S(2)}) %all-to-all-start.2) | async-done | bytes 1048608 | tf_op jit(solution)/shard_map/all_to_all | solution.py:32
  (122 shorter events, 11.7 us)
Async XLA Ops:
  1.9 94.1 %collective-permute-start.3 = (s32[1]{0:T(128)}, s32[1]{0:T(128)}, u32[]{:S(2)}, u32[]{:S(2)}) collective-permute-start(s32[1]{0:T(128)} %get-tuple-element.30), channel_id=1, source_target_pairs={{16,0},{17,1},{18,2},{19,3},{20,4},{21,5},{22,6},{23,7},{24,8},{25... | collective-permute-start | bytes 20 | tf_op jit(solution)/shard_map/ppermute | solution.py:15
  6.7 94.6 %all-to-all-start = ((bf16[32,32,1024]{2,1,0:T(8,128)(2,1)}), bf16[32,32,1024]{2,1,0:T(8,128)(2,1)S(1)}, u32[]{:S(2)}, u32[]{:S(2)}) async-start(bf16[32,32,1024]{2,1,0:T(8,128)(2,1)} %stack.12), calls=%async_computation | async-start | bytes 4194304 | tf_op jit(solution)/shard_map/all_to_all | solution.py:92
  22.1 75.3 %collective-permute-start.2 = (bf16[128,4096]{0,1:T(8,128)(2,1)}, bf16[128,4096]{0,1:T(8,128)(2,1)}, u32[]{:S(2)}, u32[]{:S(2)}) collective-permute-start(bf16[128,4096]{0,1:T(8,128)(2,1)} %bitcast.301), channel_id=1, source_target_pairs={{16,0},{17,1},{18,2},{19,3},{20,4},{21,5},{22,6},{23,7},{24,8},{25... | collective-permute-start | bytes 3145736 | tf_op jit(solution)/shard_map/ppermute | solution.py:15
  27.3 6.9 %copy-start.51 = (s32[2]{0:T(128)S(1)}, s32[2]{0:T(128)}, u32[]{:S(2)}) copy-start(s32[2]{0:T(128)} %param.11) | copy-start | bytes 28
  27.3 8.8 %copy-start.52 = (s32[2]{0:T(128)S(1)}, s32[2]{0:T(128)}, u32[]{:S(2)}) copy-start(s32[2]{0:T(128)} %param.10) | copy-start | bytes 28
  29.6 67.9 %collective-permute-start.4 = (bf16[128,4096]{0,1:T(8,128)(2,1)}, bf16[128,4096]{0,1:T(8,128)(2,1)}, u32[]{:S(2)}, u32[]{:S(2)}) collective-permute-start(bf16[128,4096]{0,1:T(8,128)(2,1)} %bitcast.302), channel_id=1, source_target_pairs={{16,0},{17,1},{18,2},{19,3},{20,4},{21,5},{22,6},{23,7},{24,8},{25... | collective-permute-start | bytes 3145736 | tf_op jit(solution)/shard_map/ppermute | solution.py:15
  32.0 65.4 %collective-permute-start = (bf16[128,1024]{1,0:T(8,128)(2,1)S(1)}, bf16[128,1024]{1,0:T(8,128)(2,1)}, u32[]{:S(2)}, u32[]{:S(2)}) collective-permute-start(bf16[128,1024]{1,0:T(8,128)(2,1)S(1)} %slice_bitcast_fusion), channel_id=1, source_target_pairs={{16,0},{17,1},{18,2},{19,3},{20,4},{21,5},{22,6},{23,7},{24,8},{25... | collective-permute-start | bytes 786440 | tf_op jit(solution)/shard_map/ppermute | solution.py:15
  34.7 59.0 %collective-permute-start.1 = (s32[1]{0:T(128)}, s32[1]{0:T(128)}, u32[]{:S(2)}, u32[]{:S(2)}) collective-permute-start(s32[1]{0:T(128)} %get-tuple-element.28), channel_id=1, source_target_pairs={{16,0},{17,1},{18,2},{19,3},{20,4},{21,5},{22,6},{23,7},{24,8},{25... | collective-permute-start | bytes 20 | tf_op jit(solution)/shard_map/ppermute | solution.py:15
  38.1 59.3 %copy-start.45 = (bf16[2,128,1024]{2,1,0:T(8,128)(2,1)S(1)}, bf16[2,128,1024]{2,1,0:T(8,128)(2,1)}, u32[]{:S(2)}) copy-start(bf16[2,128,1024]{2,1,0:T(8,128)(2,1)} %param.8) | copy-start | bytes 1572868
  107.9 3.0 %copy-start.31 = (bf16[128,1024]{0,1:T(8,128)(2,1)S(1)}, bf16[128,1024]{0,1:T(8,128)(2,1)}, u32[]{:S(2)}) copy-start(bf16[128,1024]{0,1:T(8,128)(2,1)} %get-tuple-element.24) | copy-start | bytes 786436
  110.9 1.4 copy-start
  110.9 3.2 %copy-start.20 = (f32[8,128,1152]{1,2,0:T(8,128)S(1)}, f32[8,128,1152]{1,2,0:T(8,128)}, u32[]{:S(2)}) copy-start(f32[8,128,1152]{1,2,0:T(8,128)} %get-tuple-element.39) | copy-start | bytes 14155780
  110.9 3.2 %copy-start.49 = (f32[8,128]{1,0:T(8,128)S(1)}, f32[8,128]{1,0:T(8,128)}, u32[]{:S(2)}) copy-start(f32[8,128]{1,0:T(8,128)} %get-tuple-element.38) | copy-start | bytes 12292
  114.1 1.3 copy-start.44
  115.4 1.5 copy-start.6
  122.4 3.0 %copy-start.29 = (bf16[128,1024]{0,1:T(8,128)(2,1)S(1)}, bf16[128,1024]{0,1:T(8,128)(2,1)}, u32[]{:S(2)}) copy-start(bf16[128,1024]{0,1:T(8,128)(2,1)} %get-tuple-element.27) | copy-start | bytes 786436
  125.4 1.4 copy-start.2
  125.4 3.2 %copy-start.21 = (f32[8,128,1152]{1,2,0:T(8,128)S(1)}, f32[8,128,1152]{1,2,0:T(8,128)}, u32[]{:S(2)}) copy-start(f32[8,128,1152]{1,2,0:T(8,128)} %get-tuple-element.37) | copy-start | bytes 14155780
  125.4 3.2 %copy-start.50 = (f32[8,128]{1,0:T(8,128)S(1)}, f32[8,128]{1,0:T(8,128)}, u32[]{:S(2)}) copy-start(f32[8,128]{1,0:T(8,128)} %get-tuple-element.36) | copy-start | bytes 12292
  136.9 3.3 %copy-start.27 = (bf16[128,1024]{0,1:T(8,128)(2,1)S(1)}, bf16[128,1024]{0,1:T(8,128)(2,1)}, u32[]{:S(2)}) copy-start(bf16[128,1024]{0,1:T(8,128)(2,1)} %get-tuple-element.26) | copy-start | bytes 786436
  140.1 1.4 copy-start.4
  140.2 3.2 %copy-start.19 = (f32[8,128,1152]{1,2,0:T(8,128)S(1)}, f32[8,128,1152]{1,2,0:T(8,128)}, u32[]{:S(2)}) copy-start(f32[8,128,1152]{1,2,0:T(8,128)} %get-tuple-element.35) | copy-start | bytes 14155780
  140.2 3.2 %copy-start.48 = (f32[8,128]{1,0:T(8,128)S(1)}, f32[8,128]{1,0:T(8,128)}, u32[]{:S(2)}) copy-start(f32[8,128]{1,0:T(8,128)} %get-tuple-element.34) | copy-start | bytes 12292
  143.4 1.7 copy-start.8
  143.4 2.4 copy-start.14
  143.4 2.4 copy-start.43
  145.7 1.4 copy-start.10
  145.7 1.4 copy-start.42
  147.1 2.3 copy-start.33
  147.1 2.3 copy-start.40
  148.0 1.4 copy-start.15
  153.2 3.1 %copy-start.46 = (f32[8,128]{1,0:T(8,128)}, f32[8,128]{1,0:T(8,128)S(1)}, u32[]{:S(2)}) copy-start(f32[8,128]{1,0:T(8,128)S(1)} %get-tuple-element.32) | copy-start | bytes 12292
  153.2 3.1 %copy-start.37 = (bf16[1152,128,1]{1,0,2:T(8,128)(2,1)S(1)}, bf16[1152,128,1]{1,0,2:T(8,128)(2,1)}, u32[]{:S(2)}) copy-start(bf16[1152,128,1]{1,0,2:T(8,128)(2,1)} %get-tuple-element.14) | copy-start | bytes 884740
  153.2 3.9 %copy-start.18 = (f32[8,128,1152]{1,2,0:T(8,128)S(1)}, f32[8,128,1152]{1,2,0:T(8,128)}, u32[]{:S(2)}) copy-start(f32[8,128,1152]{1,2,0:T(8,128)} %get-tuple-element.33) | copy-start | bytes 14155780
  156.3 1.1 copy-start.39
  156.4 1.1 copy-start.47
  157.5 1.7 copy-start.16
  157.5 1.7 copy-start.41
  159.2 1.4 copy-start.12
  159.2 2.5 copy-start.1
  159.2 2.5 copy-start.32
  161.7 1.7 copy-start.3
  161.7 1.7 copy-start.30
  163.3 1.7 copy-start.5
  163.3 1.7 copy-start.28
  166.8 2.1 copy-start.17
  168.9 16.3 %copy-start.7 = (bf16[8,128,1152]{1,2,0:T(8,128)(2,1)S(1)}, bf16[8,128,1152]{1,2,0:T(8,128)(2,1)}, u32[]{:S(2)}) copy-start(bf16[8,128,1152]{1,2,0:T(8,128)(2,1)} %copy-done.6) | copy-start | bytes 7077892
  168.9 61.5 %all-to-all-start.1 = ((bf16[32,32,1024]{2,1,0:T(8,128)(2,1)}), bf16[32,32,1024]{2,1,0:T(8,128)(2,1)}, u32[]{:S(2)}, u32[]{:S(2)}) async-start(bf16[32,32,1024]{2,1,0:T(8,128)(2,1)} %bitcast.283), calls=%async_computation.1 | async-start | bytes 4194304 | tf_op jit(solution)/shard_map/all_to_all | solution.py:26
  180.4 6.3 %copy-start.36 = (bf16[1152,128]{1,0:T(8,128)(2,1)S(1)}, bf16[1152,128]{1,0:T(8,128)(2,1)}, u32[]{:S(2)}) copy-start(bf16[1152,128]{1,0:T(8,128)(2,1)} %get-tuple-element.12) | copy-start | bytes 884740
  181.1 5.6 %copy-start.9 = (bf16[8,128,1152]{1,2,0:T(8,128)(2,1)S(1)}, bf16[8,128,1152]{1,2,0:T(8,128)(2,1)}, u32[]{:S(2)}) copy-start(bf16[8,128,1152]{1,2,0:T(8,128)(2,1)} %fusion.16) | copy-start | bytes 7077892
  183.1 4.2 %copy-start.11 = (bf16[8,128,1152]{1,2,0:T(8,128)(2,1)S(1)}, bf16[8,128,1152]{1,2,0:T(8,128)(2,1)}, u32[]{:S(2)}) copy-start(bf16[8,128,1152]{1,2,0:T(8,128)(2,1)} %copy-done.10) | copy-start | bytes 7077892
  183.1 4.2 %copy-start.35 = (bf16[1152,128]{1,0:T(8,128)(2,1)S(1)}, bf16[1152,128]{1,0:T(8,128)(2,1)}, u32[]{:S(2)}) copy-start(bf16[1152,128]{1,0:T(8,128)(2,1)} %get-tuple-element.13) | copy-start | bytes 884740
  183.1 56.0 %collective-permute-start.6 = (bf16[128,1024]{1,0:T(8,128)(2,1)}, bf16[128,1024]{1,0:T(8,128)(2,1)}, u32[]{:S(2)}, u32[]{:S(2)}) collective-permute-start(bf16[128,1024]{1,0:T(8,128)(2,1)} %get-tuple-element.10), channel_id=1, source_target_pairs={{16,0},{17,1},{18,2},{19,3},{20,4},{21,5},{22,6},{23,7},{24,8},{25... | collective-permute-start | bytes 786440 | tf_op jit(solution)/shard_map/ppermute | solution.py:15
  186.7 1.8 copy-start.13
  186.7 1.8 copy-start.34
  187.3 1.7 copy-start.22
  188.5 1.6 copy-start.24
  189.0 44.4 %copy-start.26 = (bf16[128,8,128]{2,0,1:T(8,128)(2,1)}, bf16[128,8,128]{2,0,1:T(8,128)(2,1)S(1)}, u32[]{:S(2)}) copy-start(bf16[128,8,128]{2,0,1:T(8,128)(2,1)S(1)} %convolution_convert_fusion) | copy-start | bytes 786436
  190.1 47.8 %copy-start.23 = (bf16[128,8,128]{2,0,1:T(8,128)(2,1)S(1)}, bf16[128,8,128]{2,0,1:T(8,128)(2,1)}, u32[]{:S(2)}) copy-start(bf16[128,8,128]{2,0,1:T(8,128)(2,1)} %copy-done.22) | copy-start | bytes 786436
  190.1 49.9 %collective-permute-start.5 = (bf16[128,4096]{0,1:T(8,128)(2,1)}, bf16[128,4096]{0,1:T(8,128)(2,1)S(1)}, u32[]{:S(2)}, u32[]{:S(2)}) collective-permute-start(bf16[128,4096]{0,1:T(8,128)(2,1)} %pad_maximum_fusion.1), channel_id=1, source_target_pairs={{16,0},{17,1},{18,2},{19,3},{20,4},{21,5},{22,6},{23,7},{24,8},{25... | collective-permute-start | bytes 3145736 | tf_op jit(solution)/shard_map/ppermute | solution.py:15
  191.5 46.4 %copy-start.25 = (bf16[128,8,128]{2,0,1:T(8,128)(2,1)S(1)}, bf16[128,8,128]{2,0,1:T(8,128)(2,1)}, u32[]{:S(2)}) copy-start(bf16[128,8,128]{2,0,1:T(8,128)(2,1)} %copy-done.24) | copy-start | bytes 786436
  233.5 5.7 %copy-start.38 = (bf16[1,128,1024]{2,1,0:T(8,128)(2,1)S(1)}, bf16[1,128,1024]{2,1,0:T(8,128)(2,1)}, u32[]{:S(2)}) copy-start(bf16[1,128,1024]{2,1,0:T(8,128)(2,1)} %get-tuple-element.9) | copy-start | bytes 786436
  233.5 20.8 %all-to-all-start.2 = ((f32[8,32,1024]{2,1,0:T(8,128)}), f32[8,32,1024]{2,1,0:T(8,128)S(1)}, u32[]{:S(2)}, u32[]{:S(2)}) async-start(f32[8,32,1024]{2,1,0:T(8,128)} %broadcast_in_dim.54), calls=%async_computation.2 | async-start | bytes 2097152 | tf_op jit(solution)/shard_map/all_to_all | solution.py:32
